TPU v7x, 256 devices: a whole 4x4x8 slice. The times are simulated.
256 devices in a mesh: seq: 64 (over y, z, core), tp: 4 (over x).
Axes of the slice: x: 4, y: 4, z: 8, core: 2. Of those that a mesh axis runs over, the one named last changes fastest.
Arguments:
- tokens: bfloat16 [24576, 1024], P(('seq', 'tp')), may hold values from -6 to 6
- w_in: bfloat16 [3, 1024, 1024], P(None, None, 'tp'), may hold values from -0.1875 to 0.1875
- short_taps: float32 [3, 3, 1024], P(None, None, 'tp'), may hold values from -3.5 to 3.5
- skip_bias: float32 [2, 1024], P(None, 'tp'), may hold values from -4 to 4
- filter_spectra: float32 [2, 2, 128, 384, 1024], P(None, None, 'seq', None, 'tp'), may hold values from -6 to 6
- w_out: bfloat16 [1024, 1024], P('tp'), may hold values from -0.1875 to 0.1875
Outputs:
- mixed_out: bfloat16 [24576, 1024], P(('seq', 'tp'))
All inputs are finite; a program needn't handle non-finite values.
Results may differ from a plain program's by a relative error of at most 0.007.
Values may be sent and summed in bfloat16 or wider, within the bound.
A program may use at most 64 MiB of HBM per device.

v0:
```python
import math

import jax
import jax.numpy as jnp
from jax import lax
from jax.sharding import PartitionSpec as P

PRECISE = lax.Precision.HIGHEST


def passed_along(array, axis, by):
    length = lax.axis_size(axis)
    pairs = [(i, i + by) for i in range(length) if 0 <= i + by < length]
    return lax.ppermute(array, axis, pairs)


def phase_table(row_count, col_count, period, direction):
    row_index = jnp.arange(row_count, dtype=jnp.int32)[:, None]
    col_index = jnp.arange(col_count, dtype=jnp.int32)[None, :]
    phases = row_index * col_index % period
    angles = direction * 2.0 * math.pi / period * phases.astype(jnp.float32)
    return (jnp.cos(angles), jnp.sin(angles))


def conjugate(pair):
    return (pair[0], -pair[1])


def product(first_pair, second_pair):
    real_part = first_pair[0] * second_pair[0] - first_pair[1] * second_pair[1]
    imag_part = first_pair[0] * second_pair[1] + first_pair[1] * second_pair[0]
    return (real_part, imag_part)


def contract(pattern, table_pair, value_pair):
    real_part = jnp.einsum(pattern, table_pair[0], value_pair[0], precision=PRECISE) - jnp.einsum(
        pattern, table_pair[1], value_pair[1], precision=PRECISE
    )
    imag_part = jnp.einsum(pattern, table_pair[0], value_pair[1], precision=PRECISE) + jnp.einsum(
        pattern, table_pair[1], value_pair[0], precision=PRECISE
    )
    return (real_part, imag_part)


def local(tokens, w_in, short_taps, skip_bias, filter_spectra, w_out):
    seq_count = lax.axis_size("seq")
    device = lax.axis_index("seq")
    blocks = 2 * seq_count
    projected = jnp.einsum(
        "rd,sdc->src",
        lax.all_gather(tokens, "tp", axis=0, tiled=True),
        w_in,
        preferred_element_type=jnp.float32,
    ).astype(jnp.bfloat16)
    positions = projected.shape[1]
    channels = projected.shape[2]
    before = passed_along(projected[:, -2:, :], "seq", 1)
    extended = jnp.concatenate([before, projected], axis=1).astype(jnp.float32)
    filtered = (
        short_taps[:, 0, None, :] * extended[:, 2:]
        + short_taps[:, 1, None, :] * extended[:, 1:-1]
        + short_taps[:, 2, None, :] * extended[:, :-2]
    )
    factor_one = max(
        (factor for factor in range(1, math.isqrt(positions) + 1) if positions % factor == 0)
    )
    factor_two = positions // factor_one
    forward_pair = phase_table(blocks, seq_count, blocks, -1.0)
    inverse_pair = phase_table(seq_count, blocks, blocks, 1.0)
    outer_table = phase_table(factor_one, factor_one, factor_one, -1.0)
    inner_table = phase_table(factor_two, factor_two, factor_two, -1.0)
    twist_pair = phase_table(factor_one, factor_two, positions, -1.0)
    twist_pair = (twist_pair[0][None, :, :, None], twist_pair[1][None, :, :, None])
    freq_index = 2 * device + jnp.arange(2, dtype=jnp.int32)[:, None]
    pos_index = jnp.arange(positions, dtype=jnp.int32)[None, :]
    angles = -2.0 * math.pi / (blocks * positions) * (freq_index * pos_index).astype(jnp.float32)
    twiddle = (jnp.cos(angles)[:, :, None], jnp.sin(angles)[:, :, None])
    carried = filtered[0]
    for order_index in range(2):
        columns = lax.all_to_all(carried[None], "seq", split_axis=1, concat_axis=0, tiled=True)
        partial_re = jnp.einsum("kp,pqc->kqc", forward_pair[0], columns, precision=PRECISE)
        partial_im = jnp.einsum("kp,pqc->kqc", forward_pair[1], columns, precision=PRECISE)
        line_pair = (
            lax.all_to_all(partial_re, "seq", split_axis=0, concat_axis=1, tiled=True),
            lax.all_to_all(partial_im, "seq", split_axis=0, concat_axis=1, tiled=True),
        )
        line_pair = product(line_pair, twiddle)
        spectrum = tuple(
            (member.reshape(2, factor_one, factor_two, channels) for member in line_pair)
        )
        spectrum = contract("ca,jabk->jcbk", outer_table, spectrum)
        spectrum = product(spectrum, twist_pair)
        spectrum = contract("db,jcbk->jdck", inner_table, spectrum)
        response = (
            filter_spectra[order_index, 0].reshape(2, factor_two, factor_one, channels),
            filter_spectra[order_index, 1].reshape(2, factor_two, factor_one, channels),
        )
        spectrum = product(spectrum, response)
        spectrum = contract("db,jdck->jcbk", conjugate(inner_table), spectrum)
        spectrum = product(spectrum, conjugate(twist_pair))
        spectrum = contract("ca,jcbk->jabk", conjugate(outer_table), spectrum)
        line_pair = tuple(
            (member.reshape(2, positions, channels) / positions for member in spectrum)
        )
        line_pair = product(line_pair, conjugate(twiddle))
        real_rows = jnp.einsum(
            "pk,kqc->pqc",
            inverse_pair[0],
            lax.all_to_all(line_pair[0], "seq", split_axis=1, concat_axis=0, tiled=True),
            precision=PRECISE,
        ) - jnp.einsum(
            "pk,kqc->pqc",
            inverse_pair[1],
            lax.all_to_all(line_pair[1], "seq", split_axis=1, concat_axis=0, tiled=True),
            precision=PRECISE,
        )
        result = lax.all_to_all(real_rows / blocks, "seq", split_axis=0, concat_axis=1, tiled=True)[
            0
        ]
        carried = filtered[order_index + 1] * (result + skip_bias[order_index] * carried)
    gated_out = carried.astype(jnp.bfloat16)
    summed = lax.psum_scatter(
        jnp.dot(gated_out, w_out, preferred_element_type=jnp.float32),
        "tp",
        scatter_dimension=0,
        tiled=True,
    )
    return summed.astype(jnp.bfloat16)


def solution(mesh):
    in_specs = (
        P(("seq", "tp"), None),
        P(None, None, "tp"),
        P(None, None, "tp"),
        P(None, "tp"),
        P(None, None, "seq", None, "tp"),
        P("tp", None),
    )
    out_specs = P(("seq", "tp"), None)
    return jax.shard_map(local, mesh=mesh, in_specs=in_specs, out_specs=out_specs, check_vma=False)
```

profile of v0, /device:TPU:1, one launch (start us, length us, event | category | flops | bytes accessed | tf_op | source)
XLA Modules:
  0.0 486.4 jit_solution(2694065401096097672)
XLA Ops:
  6.5 13.3 %all_gather.3 = bf16[384,1024]{1,0:T(8,128)(2,1)S(1)} all-gather(bf16[96,1024]{1,0:T(8,128)(2,1)} %param.6), channel_id=1, replica_groups=mesh['seq'=64,'tp'=4] {'tp'}, dimensions={0}, use_global_device_ids=true | all-gather | bytes 983040 | tf_op jit(solution)/shard_map/all_gather | solution.py:51
  21.0 5.7 %collective-permute-start = (bf16[3,2,256]{1,2,0:T(8,128)(2,1)S(1)}, bf16[3,2,256]{1,2,0:T(8,128)(2,1)S(1)}, u32[]{:S(2)}, u32[]{:S(2)}) collective-permute-start(bf16[3,2,256]{1,2,0:T(8,128)(2,1)S(1)} %slice.64), channel_id=1, source_target_pairs={{0,4},{4,8},{8,12},{12,16},{16,20},{20,24},{24,28},{28,32},{32,36}... | collective-permute-start | bytes 9224 | tf_op jit(solution)/shard_map/ppermute | solution.py:14
  26.7 2.5 collective-permute-done
  31.2 28.2 %all_to_all.186 = f32[1,384,256]{2,0,1:T(1,128)S(1)} all-to-all(f32[1,384,256]{2,0,1:T(1,128)S(1)} %copy.211), channel_id=1, replica_groups=mesh['seq'=64,'tp'=4] {'seq'}, dimensions={1} | all-to-all | bytes 786432 | tf_op jit(solution)/shard_map/all_to_all | solution.py:80
  61.4 1.5 copy.217
  62.8 6.2 %all-to-all-start.2 = ((f32[128,6,256]{2,1,0:T(8,128)}), f32[128,6,256]{2,1,0:T(8,128)S(1)}, u32[]{:S(2)}, u32[]{:S(2)}) async-start(f32[128,6,256]{2,1,0:T(8,128)} %copy.217), calls=%async_computation.2 | async-start | bytes 2097152 | tf_op jit(solution)/shard_map/all_to_all | solution.py:85
  70.0 1.5 copy.213
  71.5 26.1 %all-to-all-done.2 = f32[128,6,256]{2,1,0:T(8,128)S(1)} async-done(((f32[128,6,256]{2,1,0:T(8,128)}), f32[128,6,256]{2,1,0:T(8,128)S(1)}, u32[]{:S(2)}, u32[]{:S(2)}) %all-to-all-start.2) | async-done | bytes 786464 | tf_op jit(solution)/shard_map/all_to_all | solution.py:85
  97.6 6.4 %all-to-all-start.1 = ((f32[128,6,256]{2,1,0:T(8,128)}), f32[128,6,256]{2,1,0:T(8,128)}, u32[]{:S(2)}, u32[]{:S(2)}) async-start(f32[128,6,256]{2,1,0:T(8,128)} %copy.213), calls=%async_computation.1 | async-start | bytes 2097152 | tf_op jit(solution)/shard_map/all_to_all | solution.py:84
  108.7 3.6 fusion.401
  112.7 19.8 %all-to-all-done.1 = f32[128,6,256]{2,1,0:T(8,128)} async-done(((f32[128,6,256]{2,1,0:T(8,128)}), f32[128,6,256]{2,1,0:T(8,128)}, u32[]{:S(2)}, u32[]{:S(2)}) %all-to-all-start.1) | async-done | bytes 786464 | tf_op jit(solution)/shard_map/all_to_all | solution.py:84
  132.5 1.7 copy.214
  134.2 1.3 multiply_subtract_fusion.5
  135.4 1.3 fusion.56
  136.7 1.3 fusion.52
  138.0 1.3 fusion.11
  139.3 1.5 multiply_subtract_fusion.4
  140.8 1.3 fusion.50
  142.1 1.3 fusion.46
  143.4 1.3 fusion.9
  144.8 2.2 multiply_subtract_fusion.3
  147.0 1.3 fusion.130
  156.5 1.5 copy.248
  158.0 6.2 %all-to-all-start.3 = ((f32[2,384,256]{2,0,1:T(2,128)}), f32[2,384,256]{2,0,1:T(2,128)S(1)}, u32[]{:S(2)}, u32[]{:S(2)}) async-start(f32[2,384,256]{2,0,1:T(2,128)} %copy.248), calls=%async_computation.3 | async-start | bytes 1572864 | tf_op jit(solution)/shard_map/all_to_all | solution.py:109
  164.2 1.5 copy.250
  165.7 21.5 %all-to-all-done.3 = f32[2,384,256]{2,0,1:T(2,128)S(1)} async-done(((f32[2,384,256]{2,0,1:T(2,128)}), f32[2,384,256]{2,0,1:T(2,128)S(1)}, u32[]{:S(2)}, u32[]{:S(2)}) %all-to-all-start.3) | async-done | bytes 786464 | tf_op jit(solution)/shard_map/all_to_all | solution.py:109
  187.2 6.5 %all-to-all-start.4 = ((f32[2,384,256]{2,0,1:T(2,128)}), f32[2,384,256]{2,0,1:T(2,128)S(1)}, u32[]{:S(2)}, u32[]{:S(2)}) async-start(f32[2,384,256]{2,0,1:T(2,128)} %copy.250), calls=%async_computation.4 | async-start | bytes 1572864 | tf_op jit(solution)/shard_map/all_to_all | solution.py:114
  194.5 1.4 fusion.90
  195.9 20.6 %all-to-all-done.4 = f32[2,384,256]{2,0,1:T(2,128)S(1)} async-done(((f32[2,384,256]{2,0,1:T(2,128)}), f32[2,384,256]{2,0,1:T(2,128)S(1)}, u32[]{:S(2)}, u32[]{:S(2)}) %all-to-all-start.4) | async-done | bytes 786464 | tf_op jit(solution)/shard_map/all_to_all | solution.py:114
  219.6 6.2 %all-to-all-start.5 = ((f32[64,6,256]{2,1,0:T(8,128)}), f32[64,6,256]{2,1,0:T(8,128)S(1)}, u32[]{:S(2)}, u32[]{:S(2)}) async-start(f32[64,6,256]{2,1,0:T(8,128)} %copy.252), calls=%async_computation.5 | async-start | bytes 1048576 | tf_op jit(solution)/shard_map/all_to_all | solution.py:117
  226.3 16.7 %all-to-all-done.5 = f32[64,6,256]{2,1,0:T(8,128)S(1)} async-done(((f32[64,6,256]{2,1,0:T(8,128)}), f32[64,6,256]{2,1,0:T(8,128)S(1)}, u32[]{:S(2)}, u32[]{:S(2)}) %all-to-all-start.5) | async-done | bytes 393248 | tf_op jit(solution)/shard_map/all_to_all | solution.py:117
  244.0 20.7 %all_to_all.187 = f32[1,384,256]{2,0,1:T(1,128)S(1)} all-to-all(f32[1,384,256]{2,0,1:T(1,128)S(1)} %copy.254), channel_id=1, replica_groups=mesh['seq'=64,'tp'=4] {'seq'}, dimensions={1} | all-to-all | bytes 786432 | tf_op jit(solution)/shard_map/all_to_all | solution.py:80
  266.6 1.5 copy.256
  268.1 6.2 %all-to-all-start.7 = ((f32[128,6,256]{2,1,0:T(8,128)}), f32[128,6,256]{2,1,0:T(8,128)S(1)}, u32[]{:S(2)}, u32[]{:S(2)}) async-start(f32[128,6,256]{2,1,0:T(8,128)} %copy.256), calls=%async_computation.7 | async-start | bytes 2097152 | tf_op jit(solution)/shard_map/all_to_all | solution.py:84
  275.3 1.5 copy.259
  276.7 26.1 %all-to-all-done.7 = f32[128,6,256]{2,1,0:T(8,128)S(1)} async-done(((f32[128,6,256]{2,1,0:T(8,128)}), f32[128,6,256]{2,1,0:T(8,128)S(1)}, u32[]{:S(2)}, u32[]{:S(2)}) %all-to-all-start.7) | async-done | bytes 786464 | tf_op jit(solution)/shard_map/all_to_all | solution.py:84
  302.8 6.4 %all-to-all-start.8 = ((f32[128,6,256]{2,1,0:T(8,128)}), f32[128,6,256]{2,1,0:T(8,128)}, u32[]{:S(2)}, u32[]{:S(2)}) async-start(f32[128,6,256]{2,1,0:T(8,128)} %copy.259), calls=%async_computation.8 | async-start | bytes 2097152 | tf_op jit(solution)/shard_map/all_to_all | solution.py:85
  309.7 28.0 %all-to-all-done.8 = f32[128,6,256]{2,1,0:T(8,128)} async-done(((f32[128,6,256]{2,1,0:T(8,128)}), f32[128,6,256]{2,1,0:T(8,128)}, u32[]{:S(2)}, u32[]{:S(2)}) %all-to-all-start.8) | async-done | bytes 786464 | tf_op jit(solution)/shard_map/all_to_all | solution.py:85
  337.7 1.7 copy.260
  339.4 1.5 multiply_subtract_fusion.2
  340.9 1.3 fusion.38
  342.2 1.3 fusion.34
  343.5 1.4 fusion.5
  344.8 1.5 multiply_subtract_fusion.1
  346.3 1.3 fusion.32
  347.7 1.3 fusion.28
  349.0 1.3 fusion.3
  350.3 2.2 multiply_subtract_fusion
  361.8 1.5 copy.287
  363.3 6.2 %all-to-all-start.9 = ((f32[2,384,256]{2,0,1:T(2,128)}), f32[2,384,256]{2,0,1:T(2,128)S(1)}, u32[]{:S(2)}, u32[]{:S(2)}) async-start(f32[2,384,256]{2,0,1:T(2,128)} %copy.287), calls=%async_computation.9 | async-start | bytes 1572864 | tf_op jit(solution)/shard_map/all_to_all | solution.py:109
  369.5 1.5 copy.289
  371.0 21.5 %all-to-all-done.9 = f32[2,384,256]{2,0,1:T(2,128)S(1)} async-done(((f32[2,384,256]{2,0,1:T(2,128)}), f32[2,384,256]{2,0,1:T(2,128)S(1)}, u32[]{:S(2)}, u32[]{:S(2)}) %all-to-all-start.9) | async-done | bytes 786464 | tf_op jit(solution)/shard_map/all_to_all | solution.py:109
  392.5 6.5 %all-to-all-start.10 = ((f32[2,384,256]{2,0,1:T(2,128)}), f32[2,384,256]{2,0,1:T(2,128)S(1)}, u32[]{:S(2)}, u32[]{:S(2)}) async-start(f32[2,384,256]{2,0,1:T(2,128)} %copy.289), calls=%async_computation.10 | async-start | bytes 1572864 | tf_op jit(solution)/shard_map/all_to_all | solution.py:114
  399.0 1.1 copy.288
  400.2 1.7 all_to_all.168
  401.9 1.4 fusion.88
  403.3 18.6 %all-to-all-done.10 = f32[2,384,256]{2,0,1:T(2,128)S(1)} async-done(((f32[2,384,256]{2,0,1:T(2,128)}), f32[2,384,256]{2,0,1:T(2,128)S(1)}, u32[]{:S(2)}, u32[]{:S(2)}) %all-to-all-start.10) | async-done | bytes 786464 | tf_op jit(solution)/shard_map/all_to_all | solution.py:114
  421.9 1.2 copy.290
  423.1 1.7 all_to_all.172
  426.5 6.2 %all-to-all-start.11 = ((f32[64,6,256]{2,1,0:T(8,128)}), f32[64,6,256]{2,1,0:T(8,128)S(1)}, u32[]{:S(2)}, u32[]{:S(2)}) async-start(f32[64,6,256]{2,1,0:T(8,128)} %copy.291), calls=%async_computation.11 | async-start | bytes 1048576 | tf_op jit(solution)/shard_map/all_to_all | solution.py:117
  433.0 17.0 %all-to-all-done.11 = f32[64,6,256]{2,1,0:T(8,128)S(1)} async-done(((f32[64,6,256]{2,1,0:T(8,128)}), f32[64,6,256]{2,1,0:T(8,128)S(1)}, u32[]{:S(2)}, u32[]{:S(2)}) %all-to-all-start.11) | async-done | bytes 393248 | tf_op jit(solution)/shard_map/all_to_all | solution.py:117
  450.3 2.9 fusion.72
  453.2 24.5 %reduce-scatter.2.cloned.1.call-done = f32[96,1024]{1,0:T(8,128)} async-done(((f32[384,1024]{1,0:T(8,128)}), f32[96,1024]{1,0:T(8,128)}) %reduce-scatter.2.cloned.1.call-update) | async-done | bytes 393232 | tf_op jit(solution)/shard_map/reduce_scatter | solution.py:122
  477.7 1.7 convert_element_type.169
  (119 shorter events, 39.4 us)
Async XLA Ops:
  6.5 13.3 %copy-start = (bf16[3,1024,256]{2,1,0:T(8,128)(2,1)S(1)}, bf16[3,1024,256]{2,1,0:T(8,128)(2,1)}, u32[]{:S(2)}) copy-start(bf16[3,1024,256]{2,1,0:T(8,128)(2,1)} %param.7) | copy-start | bytes 4718596
  19.8 6.8 %copy-start.22 = (f32[3,3,256]{2,1,0:T(4,128)S(1)}, f32[3,3,256]{2,1,0:T(4,128)}, u32[]{:S(2)}) copy-start(f32[3,3,256]{2,1,0:T(4,128)} %param.8) | copy-start | bytes 27652
  21.0 8.3 %collective-permute-start = (bf16[3,2,256]{1,2,0:T(8,128)(2,1)S(1)}, bf16[3,2,256]{1,2,0:T(8,128)(2,1)S(1)}, u32[]{:S(2)}, u32[]{:S(2)}) collective-permute-start(bf16[3,2,256]{1,2,0:T(8,128)(2,1)S(1)} %slice.64), channel_id=1, source_target_pairs={{0,4},{4,8},{8,12},{12,16},{16,20},{20,24},{24,28},{28,32},{32,36}... | collective-permute-start | bytes 9224 | tf_op jit(solution)/shard_map/ppermute | solution.py:14
  62.8 34.8 %all-to-all-start.2 = ((f32[128,6,256]{2,1,0:T(8,128)}), f32[128,6,256]{2,1,0:T(8,128)S(1)}, u32[]{:S(2)}, u32[]{:S(2)}) async-start(f32[128,6,256]{2,1,0:T(8,128)} %copy.217), calls=%async_computation.2 | async-start | bytes 2097152 | tf_op jit(solution)/shard_map/all_to_all | solution.py:85
  97.6 34.9 %all-to-all-start.1 = ((f32[128,6,256]{2,1,0:T(8,128)}), f32[128,6,256]{2,1,0:T(8,128)}, u32[]{:S(2)}, u32[]{:S(2)}) async-start(f32[128,6,256]{2,1,0:T(8,128)} %copy.213), calls=%async_computation.1 | async-start | bytes 2097152 | tf_op jit(solution)/shard_map/all_to_all | solution.py:84
  132.5 1.7 copy-start.6
  132.5 1.7 copy-start.8
  138.0 1.3 copy-start.12
  143.4 1.3 copy-start.4
  143.4 1.4 copy-start.5
  149.1 0.9 copy-start.14
  149.1 0.9 copy-start.16
  155.6 0.7 copy-start.18
  158.0 29.2 %all-to-all-start.3 = ((f32[2,384,256]{2,0,1:T(2,128)}), f32[2,384,256]{2,0,1:T(2,128)S(1)}, u32[]{:S(2)}, u32[]{:S(2)}) async-start(f32[2,384,256]{2,0,1:T(2,128)} %copy.248), calls=%async_computation.3 | async-start | bytes 1572864 | tf_op jit(solution)/shard_map/all_to_all | solution.py:109
  187.2 29.4 %all-to-all-start.4 = ((f32[2,384,256]{2,0,1:T(2,128)}), f32[2,384,256]{2,0,1:T(2,128)S(1)}, u32[]{:S(2)}, u32[]{:S(2)}) async-start(f32[2,384,256]{2,0,1:T(2,128)} %copy.250), calls=%async_computation.4 | async-start | bytes 1572864 | tf_op jit(solution)/shard_map/all_to_all | solution.py:114
  216.8 1.0 copy-start.10
  218.5 7.2 %copy-start.24 = (f32[2,256]{1,0:T(2,128)S(1)}, f32[2,256]{1,0:T(2,128)}, u32[]{:S(2)}) copy-start(f32[2,256]{1,0:T(2,128)} %param.9) | copy-start | bytes 6148
  219.6 23.5 %all-to-all-start.5 = ((f32[64,6,256]{2,1,0:T(8,128)}), f32[64,6,256]{2,1,0:T(8,128)S(1)}, u32[]{:S(2)}, u32[]{:S(2)}) async-start(f32[64,6,256]{2,1,0:T(8,128)} %copy.252), calls=%async_computation.5 | async-start | bytes 1048576 | tf_op jit(solution)/shard_map/all_to_all | solution.py:117
  226.3 17.1 %copy-start.20 = (f32[1,256]{1,0:T(1,128)}, f32[1,256]{1,0:T(1,128)S(1)}, u32[]{:S(2)}) copy-start(f32[1,256]{1,0:T(1,128)S(1)} %get-tuple-element.35) | copy-start | bytes 3076
  268.1 34.8 %all-to-all-start.7 = ((f32[128,6,256]{2,1,0:T(8,128)}), f32[128,6,256]{2,1,0:T(8,128)S(1)}, u32[]{:S(2)}, u32[]{:S(2)}) async-start(f32[128,6,256]{2,1,0:T(8,128)} %copy.256), calls=%async_computation.7 | async-start | bytes 2097152 | tf_op jit(solution)/shard_map/all_to_all | solution.py:84
  302.8 34.9 %all-to-all-start.8 = ((f32[128,6,256]{2,1,0:T(8,128)}), f32[128,6,256]{2,1,0:T(8,128)}, u32[]{:S(2)}, u32[]{:S(2)}) async-start(f32[128,6,256]{2,1,0:T(8,128)} %copy.259), calls=%async_computation.8 | async-start | bytes 2097152 | tf_op jit(solution)/shard_map/all_to_all | solution.py:85
  309.6 29.7 %copy-start.7 = (f32[2,16,24]{0,2,1:T(8,128)S(1)}, f32[2,16,24]{0,2,1:T(8,128)}, u32[]{:S(2)}) copy-start(f32[2,16,24]{0,2,1:T(8,128)} %copy.215) | copy-start | bytes 9220
  337.7 1.7 copy-start.9
  343.4 1.4 copy-start.13
  349.0 1.3 copy-start.2
  349.0 1.4 copy-start.3
  354.4 0.9 copy-start.15
  354.4 0.9 copy-start.17
  360.9 0.7 copy-start.19
  363.3 29.2 %all-to-all-start.9 = ((f32[2,384,256]{2,0,1:T(2,128)}), f32[2,384,256]{2,0,1:T(2,128)S(1)}, u32[]{:S(2)}, u32[]{:S(2)}) async-start(f32[2,384,256]{2,0,1:T(2,128)} %copy.287), calls=%async_computation.9 | async-start | bytes 1572864 | tf_op jit(solution)/shard_map/all_to_all | solution.py:109
  392.5 29.4 %all-to-all-start.10 = ((f32[2,384,256]{2,0,1:T(2,128)}), f32[2,384,256]{2,0,1:T(2,128)S(1)}, u32[]{:S(2)}, u32[]{:S(2)}) async-start(f32[2,384,256]{2,0,1:T(2,128)} %copy.289), calls=%async_computation.10 | async-start | bytes 1572864 | tf_op jit(solution)/shard_map/all_to_all | solution.py:114
  423.1 1.7 copy-start.11
  426.5 23.5 %all-to-all-start.11 = ((f32[64,6,256]{2,1,0:T(8,128)}), f32[64,6,256]{2,1,0:T(8,128)S(1)}, u32[]{:S(2)}, u32[]{:S(2)}) async-start(f32[64,6,256]{2,1,0:T(8,128)} %copy.291), calls=%async_computation.11 | async-start | bytes 1048576 | tf_op jit(solution)/shard_map/all_to_all | solution.py:117
  432.7 44.9 %reduce-scatter.2.cloned.1.call-start = ((), (), s32[]{:S(2)}) async-start(), calls=%async_computation.13 | async-start | bytes 1966080 | tf_op jit(solution)/shard_map/reduce_scatter | solution.py:122
  432.8 17.4 %copy-start.21 = (f32[1,256]{1,0:T(1,128)S(1)}, f32[1,256]{1,0:T(1,128)}, u32[]{:S(2)}) copy-start(f32[1,256]{1,0:T(1,128)} %copy-done.20) | copy-start | bytes 3076
  432.9 17.4 %copy-start.23 = (f32[1,256]{1,0:T(1,128)S(1)}, f32[1,256]{1,0:T(1,128)}, u32[]{:S(2)}) copy-start(f32[1,256]{1,0:T(1,128)} %get-tuple-element.34) | copy-start | bytes 3076
  450.3 29.1 %copy-start.1 = (bf16[3,1024,256]{2,1,0:T(8,128)(2,1)S(1)}, bf16[3,1024,256]{2,1,0:T(8,128)(2,1)}, u32[]{:S(2)}) copy-start(bf16[3,1024,256]{2,1,0:T(8,128)(2,1)} %param.7) | copy-start | bytes 4718596
Sparse Core Ops, SparseCore 0:
  453.3 24.2 reduce-scatter.1
where the time goes:
time: 496 us; the launch traced here: 486 us
  waiting for transfers between devices  243 us (49%)
  starting transfers between devices  68.6 us (14%)
  blocking collectives  62.2 us (13%)
  matrix products  50.6 us (10%)
  local copies, waits for them, and re-layouts  37.5 us (8%)
  between operations  14.6 us (3%)
  other arithmetic  9.97 us (2%)
    all_to_all x2, waiting for transfers between devices, local(): lax.all_to_all(partial_im, 'seq', split_axis=0, concat_axis=1, tiled=True)  54.1 us
    all_to_all x2, blocking collectives, local(): lax.all_to_all(carried[None], 'seq', split_axis=1, concat_axis=0, tiled=T...  48.9 us
    all_to_all x2, waiting for transfers between devices, local(): lax.all_to_all(partial_re, 'seq', split_axis=0, concat_axis=1, tiled=True)  45.9 us
    all_to_all x2, waiting for transfers between devices, local(): lax.all_to_all(line_pair[0], 'seq', split_axis=1, concat_axis=0, tiled=True)  42.9 us
    all_to_all x2, waiting for transfers between devices, local(): lax.all_to_all(line_pair[1], 'seq', split_axis=1, concat_axis=0, tiled=True)  39.3 us
    all_to_all x2, waiting for transfers between devices, local(): lax.all_to_all(real_rows / blocks, 'seq', split_axis=0, concat_axis=1, ti...  33.7 us
    reduce_scatter x1, waiting for transfers between devices, local(): lax.psum_scatter(jnp.dot(gated_out, w_out, preferred_element_type=jnp.flo...  24.5 us
    all_gather x1, blocking collectives, local(): lax.all_gather(tokens, 'tp', axis=0, tiled=True)  13.3 us
  transfers between devices with their start and end apart: 12, of which 12 were waited for; matrix products, arithmetic and copies ran while one was open for 5% of the time, Pallas kernels for 0%

commit v1 on v0

v1 whole, which is shorter than its diff:
```python
import math

import jax
import jax.numpy as jnp
import ml_dtypes
import numpy as np
from jax import lax
from jax.experimental import pallas as pl
from jax.experimental.pallas import tpu as pltpu
from jax.sharding import PartitionSpec as P

MESH = pl.DeviceIdType.MESH
BF = jnp.bfloat16
F32 = jnp.float32
SEQ, TP = 64, 4
ROWS, CH, OUT_ROWS = 384, 256, 96
RES = 128
NT = (((1,), (1,)), ((), ()))
NN = (((1,), (0,)), ((), ()))


def halves(table):
    high = table.astype(ml_dtypes.bfloat16)
    low = (table - high.astype(np.float64)).astype(ml_dtypes.bfloat16)
    return high, low


def tables():
    total = RES * ROWS
    line = np.arange(ROWS)
    inner = 2.0 * np.pi / ROWS * (np.outer(line, line) % ROWS)
    cos_hi, cos_lo = halves(np.cos(inner))
    sin_hi, sin_lo = halves(np.sin(inner))
    inner_table = np.stack([cos_hi, sin_hi, cos_lo, sin_lo])
    order = np.concatenate([2 * np.arange(SEQ), 2 * np.arange(SEQ) + 1])
    outer = 2.0 * np.pi / RES * (np.outer(order, np.arange(SEQ)) % RES)
    first = np.concatenate([np.cos(outer), -np.sin(outer)], axis=0)
    first_hi, first_lo = halves(first)
    first_table = np.concatenate([first_hi, first_hi, first_lo], axis=1)
    last = np.concatenate([np.cos(outer.T), -np.sin(outer.T)], axis=1) / total
    last_hi, last_lo = halves(last)
    last_table = np.concatenate([last_hi, last_hi, last_lo], axis=1)
    angle = -2.0 * np.pi / total * np.outer(order, line)
    twist = np.stack([np.cos(angle), np.sin(angle)]).astype(np.float32)
    pick = np.zeros((512, 512), ml_dtypes.bfloat16)
    for dest in range(SEQ):
        for slot in range(4):
            for low in range(2):
                pick[dest * 8 + slot * 2 + low, slot * 128 + low * 64 + dest] = 1
    return inner_table, first_table, last_table, twist, pick


def split(value):
    high = value.astype(BF)
    low = (value - high.astype(F32)).astype(BF)
    return high, low


def dot(a, b, dims=NN):
    return lax.dot_general(a, b, dims, preferred_element_type=F32)


def body(
    tok, w_in, taps_s, taps_v, bias_s, spec, w_out, inner_c, first_c, last_c, twist_c, pick_c,
    out,
    spec_v, w_in_v, inner_v, wmat, tg, wg, h_send, h_recv, f_send, f_recv, u_send, u_recv,
    wide, f2_v, halo, g_send, g_recv,
    load_sem, own_sem, tok_s, tok_r, wo_s, wo_r, h_s, h_r, f_s, f_r, halo_s, halo_r, u_s, u_r, g_s, g_r,
):
    me = lax.axis_index("seq")
    mx = lax.axis_index("tp")
    my_y = me // 16
    my_z = (me // 2) % 8
    my_c = me % 2

    def peer(i):
        return ((my_y + i // 16) % 4) * 16 + ((my_z + (i // 2) % 8) % 8) * 2 + (my_c + i % 2) % 2

    def loads(k):
        pairs = ((spec.at[0], spec_v.at[0]), (w_in, w_in_v), (spec.at[1], spec_v.at[1]), (inner_c, inner_v))
        return pltpu.make_async_copy(pairs[k][0], pairs[k][1], load_sem.at[k])

    for k in range(4):
        loads(k).start()

    barrier = pltpu.get_barrier_semaphore()

    def greet(i, carry):
        pl.semaphore_signal(barrier, inc=1, device_id={"seq": peer(i)}, device_id_type=MESH)
        return carry

    lax.fori_loop(1, SEQ, greet, 0)
    for t in range(1, TP):
        pl.semaphore_signal(barrier, inc=1, device_id={"tp": (mx + t) % TP}, device_id_type=MESH)
    pl.semaphore_wait(barrier, SEQ - 1 + TP - 1)

    def x_copy(src, dst, ssem, rsem, t):
        return pltpu.make_async_remote_copy(
            src, dst, ssem, rsem, device_id={"tp": (mx + t) % TP}, device_id_type=MESH
        )

    def own_copy(src, dst, k):
        return pltpu.make_async_copy(src, dst, own_sem.at[k])

    def all_wait(src_slice, dst_slice, ssem, rsem):
        pltpu.make_async_copy(src_slice, src_slice, ssem).wait()
        pltpu.make_async_copy(dst_slice, dst_slice, rsem).wait()

    for t in range(1, TP):
        x_copy(tok, tg.at[mx], tok_s, tok_r, t).start()
    own_copy(tok, tg.at[mx], 0).start()

    def spread(send, recv, ssem, rsem, k):
        def one(i, carry):
            to = peer(i)
            pltpu.make_async_remote_copy(
                send.at[to], recv.at[me], ssem, rsem, device_id={"seq": to}, device_id_type=MESH
            ).start()
            return carry

        lax.fori_loop(1, SEQ, one, 0)
        own_copy(send.at[me], recv.at[me], k).start()

    def gathered(send, recv, ssem, rsem, k):
        own_copy(send.at[me], recv.at[me], k).wait()
        pltpu.make_async_copy(recv.at[pl.ds(0, SEQ - 1)], recv.at[pl.ds(0, SEQ - 1)], rsem).wait()

    def sent(send, ssem):
        pltpu.make_async_copy(send.at[pl.ds(0, SEQ - 1)], send.at[pl.ds(0, SEQ - 1)], ssem).wait()

    def ship_filter(o, g):
        k = 2 * o + g
        lanes = slice(128 * g, 128 * g + 128)
        line = jnp.concatenate(
            [spec_v[o, ri, j, :, lanes].astype(BF) for ri in range(2) for j in range(2)], axis=1
        )
        turned = dot(pick_c[...], line, NT)
        h_send[k] = turned.reshape(SEQ, 8, ROWS).astype(BF)
        spread(h_send.at[k], h_recv.at[k], h_s.at[k], h_r.at[k], 4 + k)

    loads(0).wait()
    ship_filter(0, 0)
    ship_filter(0, 1)

    for t in range(1, TP):
        x_copy(w_out, wg.at[mx], wo_s, wo_r, t).start()
    own_copy(w_out, wg.at[mx], 1).start()

    loads(1).wait()
    own_copy(tok, tg.at[mx], 0).wait()
    pltpu.make_async_copy(tg.at[pl.ds(0, 3)], tg.at[pl.ds(0, 3)], tok_r).wait()
    rows = tg[...].reshape(ROWS, 1024)
    lines = [dot(rows, w_in_v[b]).astype(BF) for b in range(3)]
    turned = dot(pick_c[...], jnp.concatenate(lines[:2], axis=1), NT)
    f_send[...] = turned.reshape(SEQ, 8, ROWS).astype(BF)
    spread(f_send, f_recv, f_s, f_r, 2)
    f2_v[...] = lines[2]
    after = (me + 1) % SEQ
    edge = pltpu.make_async_remote_copy(
        f2_v.at[pl.ds(ROWS - 16, 16)], halo, halo_s, halo_r, device_id={"seq": after}, device_id_type=MESH
    )
    edge.start()

    loads(2).wait()
    ship_filter(1, 0)
    ship_filter(1, 1)

    loads(3).wait()
    for part in range(2):
        cos_t = inner_v[2 * part]
        sin_t = inner_v[2 * part + 1]
        wmat[part, 0:ROWS, 0:ROWS] = cos_t
        wmat[part, ROWS:, ROWS:] = cos_t
        wmat[part, ROWS:, 0:ROWS] = sin_t
        wmat[part, 0:ROWS, ROWS:] = -sin_t

    def thrice(value, dims):
        high, low = split(value)
        return dot(high, wmat[0], dims) + dot(low, wmat[0], dims) + dot(high, wmat[1], dims)

    def stacked(value):
        high, low = split(value)
        return jnp.concatenate([high, low, high], axis=0)

    def convolve(pair, k):
        wide[...] = h_recv[k].astype(F32)
        z = dot(first_c[...], stacked(jnp.concatenate(pair, axis=1)))
        tr, ti = twist_c[0], twist_c[1]
        blocks = []
        for low in range(2):
            cols = slice(ROWS * low, ROWS * low + ROWS)
            zr, zi = z[:RES, cols], z[RES:, cols]
            blocks.append(jnp.concatenate([zr * tr - zi * ti, zr * ti + zi * tr], axis=1))
        x = thrice(jnp.concatenate(blocks, axis=0), NN)
        blocks = []
        for low in range(2):
            for j in range(2):
                at = low * RES + j * SEQ
                xr, xi = x[at : at + SEQ, :ROWS], x[at : at + SEQ, ROWS:]
                hr = wide[:, j * 2 + low, :]
                hi = wide[:, (2 + j) * 2 + low, :]
                blocks.append(jnp.concatenate([xr * hr - xi * hi, xr * hi + xi * hr], axis=1))
        v = thrice(jnp.concatenate(blocks, axis=0), NT)
        real, imag = [], []
        for low in range(2):
            vr, vi = v[RES * low : RES * low + RES, :ROWS], v[RES * low : RES * low + RES, ROWS:]
            real.append(vr * tr + vi * ti)
            imag.append(vi * tr - vr * ti)
        rhs = jnp.concatenate([jnp.concatenate(real, axis=1), jnp.concatenate(imag, axis=1)], axis=0)
        y = dot(last_c[...], stacked(rhs))
        return [y[:, :ROWS], y[:, ROWS:]]

    at_row = lax.broadcasted_iota(jnp.int32, (SEQ, ROWS), 0)
    at_col = lax.broadcasted_iota(jnp.int32, (SEQ, ROWS), 1)

    def delayed(x, by):
        turned = pltpu.roll(x, by, 1)
        fix = jnp.where(at_row == 0, 0.0, pltpu.roll(turned, 1, 0))
        return jnp.where(at_col < by, fix, turned)

    def filtered(b, i):
        x = wide[:, b * 4 + i, :]
        col = 64 * i + me
        return taps_s[b, 0, col] * x + taps_s[b, 1, col] * delayed(x, 1) + taps_s[b, 2, col] * delayed(x, 2)

    gathered(f_send, f_recv, f_s, f_r, 2)
    wide[...] = f_recv[...].astype(F32)
    values = [filtered(0, i) for i in range(4)]
    gates = [filtered(1, i) for i in range(4)]
    carried = []
    for g in range(2):
        gathered(h_send.at[g], h_recv.at[g], h_s.at[g], h_r.at[g], 4 + g)
        ys = convolve(values[2 * g : 2 * g + 2], g)
        for low in range(2):
            i = 2 * g + low
            carried.append(gates[i] * (ys[low] + bias_s[0, 64 * i + me] * values[i]))
    ends = []
    for g in range(2):
        k = 2 + g
        gathered(h_send.at[k], h_recv.at[k], h_s.at[k], h_r.at[k], 4 + k)
        ys = convolve(carried[2 * g : 2 * g + 2], k)
        for low in range(2):
            i = 2 * g + low
            ends.append(ys[low] + bias_s[1, 64 * i + me] * carried[i])
    for i in range(4):
        wide[:, i, :] = ends[i]
    u_send[...] = wide[:, 0:4, :].astype(BF)
    spread(u_send, u_recv, u_s, u_r, 3)

    edge.wait()
    x = f2_v[...].astype(F32)
    edge_rows = jnp.where(me > 0, halo[...].astype(F32), 0.0)
    at = lax.broadcasted_iota(jnp.int32, (ROWS, CH), 0)
    one = jnp.where(at == 0, edge_rows[15:16], pltpu.roll(x, 1, 0))
    two = jnp.where(at == 0, edge_rows[14:15], jnp.where(at == 1, edge_rows[15:16], pltpu.roll(x, 2, 0)))
    gate = taps_v[2, 0:1, :] * x + taps_v[2, 1:2, :] * one + taps_v[2, 2:3, :] * two

    gathered(u_send, u_recv, u_s, u_r, 3)
    wide[:, 0:4, :] = u_recv[...].astype(F32)
    turned = jnp.concatenate([wide[:, i, :] for i in range(4)], axis=0).T
    g_send[...] = (gate * turned).astype(BF).reshape(TP, OUT_ROWS, CH)
    for t in range(1, TP):
        x_copy(g_send.at[(mx + t) % TP], g_recv.at[mx], g_s, g_r, t).start()
    own_copy(g_send.at[mx], g_recv.at[mx], 8).start()
    own_copy(w_out, wg.at[mx], 1).wait()
    pltpu.make_async_copy(wg.at[pl.ds(0, 3)], wg.at[pl.ds(0, 3)], wo_r).wait()
    own_copy(g_send.at[mx], g_recv.at[mx], 8).wait()
    pltpu.make_async_copy(g_recv.at[pl.ds(0, 3)], g_recv.at[pl.ds(0, 3)], g_r).wait()
    total = dot(g_recv[0], wg[0])
    for t in range(1, TP):
        total = total + dot(g_recv[t], wg[t])
    out[...] = total.astype(BF)

    pltpu.make_async_copy(tg.at[pl.ds(0, 3)], tg.at[pl.ds(0, 3)], tok_s).wait()
    pltpu.make_async_copy(wg.at[pl.ds(0, 3)], wg.at[pl.ds(0, 3)], wo_s).wait()
    for k in range(4):
        sent(h_send.at[k], h_s.at[k])
    sent(f_send, f_s)
    sent(u_send, u_s)
    pltpu.make_async_copy(g_send.at[pl.ds(0, 3)], g_send.at[pl.ds(0, 3)], g_s).wait()


def local(tokens, w_in, short_taps, skip_bias, filter_spectra, w_out):
    inner_table, first_table, last_table, twist, pick = tables()
    vmem = pl.BlockSpec(memory_space=pltpu.VMEM)
    smem = pl.BlockSpec(memory_space=pltpu.SMEM)
    hbm = pl.BlockSpec(memory_space=pl.ANY)
    dma = pltpu.SemaphoreType.DMA
    return pl.pallas_call(
        body,
        out_shape=jax.ShapeDtypeStruct((OUT_ROWS, 1024), BF),
        in_specs=[vmem, hbm, smem, vmem, smem, hbm, hbm, hbm, vmem, vmem, vmem, vmem],
        out_specs=vmem,
        scratch_shapes=[
            pltpu.VMEM((2, 2, 2, ROWS, CH), F32),
            pltpu.VMEM((3, 1024, CH), BF),
            pltpu.VMEM((4, ROWS, ROWS), BF),
            pltpu.VMEM((2, 2 * ROWS, 2 * ROWS), BF),
            pltpu.VMEM((TP, OUT_ROWS, 1024), BF),
            pltpu.VMEM((TP, CH, 1024), BF),
            pltpu.VMEM((4, SEQ, 8, ROWS), BF),
            pltpu.VMEM((4, SEQ, 8, ROWS), BF),
            pltpu.VMEM((SEQ, 8, ROWS), BF),
            pltpu.VMEM((SEQ, 8, ROWS), BF),
            pltpu.VMEM((SEQ, 4, ROWS), BF),
            pltpu.VMEM((SEQ, 4, ROWS), BF),
            pltpu.VMEM((SEQ, 8, ROWS), F32),
            pltpu.VMEM((ROWS, CH), BF),
            pltpu.VMEM((16, CH), BF),
            pltpu.VMEM((TP, OUT_ROWS, CH), BF),
            pltpu.VMEM((TP, OUT_ROWS, CH), BF),
            dma((4,)),
            dma((9,)),
            dma, dma, dma, dma,
            dma((4,)),
            dma((4,)),
            dma, dma, dma, dma, dma, dma, dma, dma,
        ],
        compiler_params=pltpu.CompilerParams(
            collective_id=0, has_side_effects=True, vmem_limit_bytes=60 * 1024 * 1024
        ),
    )(
        tokens, w_in, short_taps, short_taps, skip_bias, filter_spectra, w_out,
        jnp.asarray(inner_table), jnp.asarray(first_table), jnp.asarray(last_table),
        jnp.asarray(twist), jnp.asarray(pick),
    )


def solution(mesh):
    in_specs = (
        P(("seq", "tp"), None),
        P(None, None, "tp"),
        P(None, None, "tp"),
        P(None, "tp"),
        P(None, None, "seq", None, "tp"),
        P("tp", None),
    )
    out_specs = P(("seq", "tp"), None)
    return jax.shard_map(local, mesh=mesh, in_specs=in_specs, out_specs=out_specs, check_vma=False)
```

time: 496 us -> 82.9 us (0.17); the launches traced: 486 us -> 82.7 us
  waiting for transfers between devices: 243 us -> 0 us
  Pallas kernels: 0 us -> 81.1 us
  starting transfers between devices: 68.6 us -> 0 us
  blocking collectives: 62.2 us -> 0 us
  matrix products: 50.6 us -> 0 us
  local copies, waits for them, and re-layouts: 37.5 us -> 1.62 us
  between operations: 14.6 us -> 0.01 us
  other arithmetic: 9.97 us -> 0 us
    all_to_all x10 -> x0, waiting for transfers between devices: 216 us -> none  [the longest x2 54.1 us: local(): lax.all_to_all(partial_im, 'seq', split_axis=0, concat_axis=1, tiled=True)]
    pallas_call x0 -> x1, Pallas kernels: none -> 81.1 us  [local(): pl.pallas_call(body, out_shape=jax.ShapeDtypeStruct((OUT_ROWS, 1024), BF)...]
    all_to_all x10 -> x0, starting transfers between devices: 62.9 us -> none  [the longest x2 13 us: local(): lax.all_to_all(line_pair[1], 'seq', split_axis=1, concat_axis=0, tiled=True)]
    dot_general x42 -> x0, matrix products: 50.6 us -> none  [the longest x8 11 us: contract(): jnp.einsum(pattern, table_pair[1], value_pair[0], precision=PRECISE)]
    all_to_all x2 -> x0, blocking collectives: 48.9 us -> none  [local(): lax.all_to_all(carried[None], 'seq', split_axis=1, concat_axis=0, tiled=T...]
    reduce_scatter x1 -> x0, waiting for transfers between devices: 24.5 us -> none  [local(): lax.psum_scatter(jnp.dot(gated_out, w_out, preferred_element_type=jnp.flo...]
    all_gather x1 -> x0, blocking collectives: 13.3 us -> none  [local(): lax.all_gather(tokens, 'tp', axis=0, tiled=True)]
    all_to_all x14 -> x0, local copies, waits for them, and re-layouts: 11.6 us -> none  [the longest x4 3.71 us: local(): lax.all_to_all(line_pair[1], 'seq', split_axis=1, concat_axis=0, tiled=True)]
  transfers between devices with their start and end apart: 12 -> 0, of which waited for: 12 -> 0; matrix products, arithmetic and copies ran while one was open for 5% -> 0% of each run, Pallas kernels for 0% -> 0%
where the time goes in v1:
time: 82.9 us; the launch traced here: 82.7 us
  Pallas kernels  81.1 us (98%)
  local copies, waits for them, and re-layouts  1.62 us (2%)
    pallas_call x1, Pallas kernels, local(): pl.pallas_call(body, out_shape=jax.ShapeDtypeStruct((OUT_ROWS, 1024), BF)...  81.1 us

profile of v1, /device:TPU:1, one launch (start us, length us, event | category | flops | bytes accessed | tf_op | source)
XLA Modules:
  0.0 82.7 jit_solution(18287026417804616307)
XLA Ops:
  0.0 81.1 %shard_map.109 = bf16[96,1024]{1,0:T(8,128)(2,1)} custom-call(bf16[96,1024]{1,0:T(8,128)(2,1)} %tok.1, bf16[3,1024,256]{2,1,0:T(8,128)(2,1)} %w_in.1, f32[3,3,256]{2,1,0:T(4,128)} %taps_v.1, f32[3,3,256]{2,1,0:T(4,128)} %taps_v.1, f32[2,256]{1,0:T(2,128)} %bias_s.1, f32[2,2,2,384,256]{4,3,2,1,0:T(8,128)} %spec.1, bf16[256,1024]{1,0:T(8,128)(2,1)} %w_out.1, ...), custom_call_target="tpu_custom_call" | custom-call | tf_op jit(solution)/shard_map/pallas_call | solution.py:289
  81.1 1.6 %copy.13 = bf16[96,1024]{1,0:T(8,128)(2,1)} copy(bf16[96,1024]{1,0:T(8,128)(2,1)} %shard_map.109) | data formatting | bytes 393216

commit v2 on v1

--- a/solution.py
+++ b/solution.py
@@ -61,27 +61,18 @@
 
 
 def body(
-    tok, w_in, taps_s, taps_v, bias_s, spec, w_out, inner_c, first_c, last_c, twist_c, pick_c,
+    tok, w_in, taps_h, bias_h, spec, w_out, inner_h, first_h, last_h, twist_h, pick_h,
     out,
-    spec_v, w_in_v, inner_v, wmat, tg, wg, h_send, h_recv, f_send, f_recv, u_send, u_recv,
-    wide, f2_v, halo, g_send, g_recv,
+    taps_s, bias_s, taps_v, first_c, last_c, twist_c, pick_c, spec_v, w_in_v, inner_v, wmat, tg, wg, h_send, h_recv, f_send, f_recv, u_send, u_recv,
+    wide, f2_v, halo, gate_v, g_send, g_recv,
     load_sem, own_sem, tok_s, tok_r, wo_s, wo_r, h_s, h_r, f_s, f_r, halo_s, halo_r, u_s, u_r, g_s, g_r,
 ):
     me = lax.axis_index("seq")
     mx = lax.axis_index("tp")
-    my_y = me // 16
-    my_z = (me // 2) % 8
-    my_c = me % 2
 
     def peer(i):
-        return ((my_y + i // 16) % 4) * 16 + ((my_z + (i // 2) % 8) % 8) * 2 + (my_c + i % 2) % 2
-
-    def loads(k):
-        pairs = ((spec.at[0], spec_v.at[0]), (w_in, w_in_v), (spec.at[1], spec_v.at[1]), (inner_c, inner_v))
-        return pltpu.make_async_copy(pairs[k][0], pairs[k][1], load_sem.at[k])
-
-    for k in range(4):
-        loads(k).start()
+        to = me + i
+        return jnp.where(to >= SEQ, to - SEQ, to)
 
     barrier = pltpu.get_barrier_semaphore()
 
@@ -92,7 +83,17 @@
     lax.fori_loop(1, SEQ, greet, 0)
     for t in range(1, TP):
         pl.semaphore_signal(barrier, inc=1, device_id={"tp": (mx + t) % TP}, device_id_type=MESH)
-    pl.semaphore_wait(barrier, SEQ - 1 + TP - 1)
+
+    def loads(k):
+        pairs = (
+            (spec.at[0], spec_v.at[0]), (pick_h, pick_c), (w_in, w_in_v), (spec.at[1], spec_v.at[1]),
+            (inner_h, inner_v), (first_h, first_c), (twist_h, twist_c), (last_h, last_c),
+            (taps_h, taps_v), (taps_h, taps_s), (bias_h, bias_s),
+        )
+        return pltpu.make_async_copy(pairs[k][0], pairs[k][1], load_sem.at[k])
+
+    for k in range(11):
+        loads(k).start()
 
     def x_copy(src, dst, ssem, rsem, t):
         return pltpu.make_async_remote_copy(
@@ -105,10 +106,6 @@
     def all_wait(src_slice, dst_slice, ssem, rsem):
         pltpu.make_async_copy(src_slice, src_slice, ssem).wait()
         pltpu.make_async_copy(dst_slice, dst_slice, rsem).wait()
-
-    for t in range(1, TP):
-        x_copy(tok, tg.at[mx], tok_s, tok_r, t).start()
-    own_copy(tok, tg.at[mx], 0).start()
 
     def spread(send, recv, ssem, rsem, k):
         def one(i, carry):
@@ -128,7 +125,7 @@
     def sent(send, ssem):
         pltpu.make_async_copy(send.at[pl.ds(0, SEQ - 1)], send.at[pl.ds(0, SEQ - 1)], ssem).wait()
 
-    def ship_filter(o, g):
+    def turn_filter(o, g):
         k = 2 * o + g
         lanes = slice(128 * g, 128 * g + 128)
         line = jnp.concatenate(
@@ -136,17 +133,26 @@
         )
         turned = dot(pick_c[...], line, NT)
         h_send[k] = turned.reshape(SEQ, 8, ROWS).astype(BF)
+
+    def ship_filter(k):
         spread(h_send.at[k], h_recv.at[k], h_s.at[k], h_r.at[k], 4 + k)
 
     loads(0).wait()
-    ship_filter(0, 0)
-    ship_filter(0, 1)
+    loads(1).wait()
+    turn_filter(0, 0)
+    turn_filter(0, 1)
+    pl.semaphore_wait(barrier, SEQ - 1 + TP - 1)
+    for t in range(1, TP):
+        x_copy(tok, tg.at[mx], tok_s, tok_r, t).start()
+    own_copy(tok, tg.at[mx], 0).start()
+    ship_filter(0)
+    ship_filter(1)
 
     for t in range(1, TP):
         x_copy(w_out, wg.at[mx], wo_s, wo_r, t).start()
     own_copy(w_out, wg.at[mx], 1).start()
 
-    loads(1).wait()
+    loads(2).wait()
     own_copy(tok, tg.at[mx], 0).wait()
     pltpu.make_async_copy(tg.at[pl.ds(0, 3)], tg.at[pl.ds(0, 3)], tok_r).wait()
     rows = tg[...].reshape(ROWS, 1024)
@@ -161,11 +167,13 @@
     )
     edge.start()
 
-    loads(2).wait()
-    ship_filter(1, 0)
-    ship_filter(1, 1)
-
     loads(3).wait()
+    for g in range(2):
+        turn_filter(1, g)
+        ship_filter(2 + g)
+
+    for k in range(4, 11):
+        loads(k).wait()
     for part in range(2):
         cos_t = inner_v[2 * part]
         sin_t = inner_v[2 * part + 1]
@@ -182,16 +190,20 @@
         high, low = split(value)
         return jnp.concatenate([high, low, high], axis=0)
 
-    def convolve(pair, k):
-        wide[...] = h_recv[k].astype(F32)
+    tr, ti = twist_c[0], twist_c[1]
+
+    def forward(pair):
         z = dot(first_c[...], stacked(jnp.concatenate(pair, axis=1)))
-        tr, ti = twist_c[0], twist_c[1]
         blocks = []
         for low in range(2):
             cols = slice(ROWS * low, ROWS * low + ROWS)
             zr, zi = z[:RES, cols], z[RES:, cols]
             blocks.append(jnp.concatenate([zr * tr - zi * ti, zr * ti + zi * tr], axis=1))
-        x = thrice(jnp.concatenate(blocks, axis=0), NN)
+        return thrice(jnp.concatenate(blocks, axis=0), NN)
+
+    def inverse(x, k):
+        gathered(h_send.at[k], h_recv.at[k], h_s.at[k], h_r.at[k], 4 + k)
+        wide[...] = h_recv[k].astype(F32)
         blocks = []
         for low in range(2):
             for j in range(2):
@@ -227,25 +239,14 @@
     wide[...] = f_recv[...].astype(F32)
     values = [filtered(0, i) for i in range(4)]
     gates = [filtered(1, i) for i in range(4)]
+    spectra = [forward(values[2 * g : 2 * g + 2]) for g in range(2)]
     carried = []
     for g in range(2):
-        gathered(h_send.at[g], h_recv.at[g], h_s.at[g], h_r.at[g], 4 + g)
-        ys = convolve(values[2 * g : 2 * g + 2], g)
+        ys = inverse(spectra[g], g)
         for low in range(2):
             i = 2 * g + low
             carried.append(gates[i] * (ys[low] + bias_s[0, 64 * i + me] * values[i]))
-    ends = []
-    for g in range(2):
-        k = 2 + g
-        gathered(h_send.at[k], h_recv.at[k], h_s.at[k], h_r.at[k], 4 + k)
-        ys = convolve(carried[2 * g : 2 * g + 2], k)
-        for low in range(2):
-            i = 2 * g + low
-            ends.append(ys[low] + bias_s[1, 64 * i + me] * carried[i])
-    for i in range(4):
-        wide[:, i, :] = ends[i]
-    u_send[...] = wide[:, 0:4, :].astype(BF)
-    spread(u_send, u_recv, u_s, u_r, 3)
+        spectra[g] = forward(carried[2 * g : 2 * g + 2])
 
     edge.wait()
     x = f2_v[...].astype(F32)
@@ -253,74 +254,93 @@
     at = lax.broadcasted_iota(jnp.int32, (ROWS, CH), 0)
     one = jnp.where(at == 0, edge_rows[15:16], pltpu.roll(x, 1, 0))
     two = jnp.where(at == 0, edge_rows[14:15], jnp.where(at == 1, edge_rows[15:16], pltpu.roll(x, 2, 0)))
-    gate = taps_v[2, 0:1, :] * x + taps_v[2, 1:2, :] * one + taps_v[2, 2:3, :] * two
-
-    gathered(u_send, u_recv, u_s, u_r, 3)
-    wide[:, 0:4, :] = u_recv[...].astype(F32)
-    turned = jnp.concatenate([wide[:, i, :] for i in range(4)], axis=0).T
-    g_send[...] = (gate * turned).astype(BF).reshape(TP, OUT_ROWS, CH)
-    for t in range(1, TP):
-        x_copy(g_send.at[(mx + t) % TP], g_recv.at[mx], g_s, g_r, t).start()
-    own_copy(g_send.at[mx], g_recv.at[mx], 8).start()
+    gate_v[...] = taps_v[2, 0:1, :] * x + taps_v[2, 1:2, :] * one + taps_v[2, 2:3, :] * two
+
+    for g in range(2):
+        ys = inverse(spectra[g], 2 + g)
+        for low in range(2):
+            i = 2 * g + low
+            wide[:, low, :] = ys[low] + bias_s[1, 64 * i + me] * carried[i]
+        u_send[g] = wide[:, 0:2, :].astype(BF)
+        spread(u_send.at[g], u_recv.at[g], u_s.at[g], u_r.at[g], 8 + g)
+
+    for g in range(2):
+        gathered(u_send.at[g], u_recv.at[g], u_s.at[g], u_r.at[g], 8 + g)
+        wide[:, 0:2, :] = u_recv[g].astype(F32)
+        turned = jnp.concatenate([wide[:, low, :] for low in range(2)], axis=0).T
+        lanes = slice(128 * g, 128 * g + 128)
+        g_send[g] = (gate_v[:, lanes] * turned).astype(BF).reshape(TP, OUT_ROWS, 128)
+        for t in range(1, TP):
+            x_copy(g_send.at[g, (mx + t) % TP], g_recv.at[g, mx], g_s.at[g], g_r.at[g], t).start()
+        own_copy(g_send.at[g, mx], g_recv.at[g, mx], 10 + g).start()
     own_copy(w_out, wg.at[mx], 1).wait()
     pltpu.make_async_copy(wg.at[pl.ds(0, 3)], wg.at[pl.ds(0, 3)], wo_r).wait()
-    own_copy(g_send.at[mx], g_recv.at[mx], 8).wait()
-    pltpu.make_async_copy(g_recv.at[pl.ds(0, 3)], g_recv.at[pl.ds(0, 3)], g_r).wait()
-    total = dot(g_recv[0], wg[0])
-    for t in range(1, TP):
-        total = total + dot(g_recv[t], wg[t])
-    out[...] = total.astype(BF)
+    parts = []
+    for g in range(2):
+        own_copy(g_send.at[g, mx], g_recv.at[g, mx], 10 + g).wait()
+        pltpu.make_async_copy(g_recv.at[g, pl.ds(0, 3)], g_recv.at[g, pl.ds(0, 3)], g_r.at[g]).wait()
+        line = jnp.concatenate([g_recv[g, t] for t in range(TP)], axis=1)
+        parts.append(dot(line, wg[:, g].reshape(512, 1024)))
+    out[...] = (parts[0] + parts[1]).astype(BF)
 
     pltpu.make_async_copy(tg.at[pl.ds(0, 3)], tg.at[pl.ds(0, 3)], tok_s).wait()
     pltpu.make_async_copy(wg.at[pl.ds(0, 3)], wg.at[pl.ds(0, 3)], wo_s).wait()
     for k in range(4):
         sent(h_send.at[k], h_s.at[k])
     sent(f_send, f_s)
-    sent(u_send, u_s)
-    pltpu.make_async_copy(g_send.at[pl.ds(0, 3)], g_send.at[pl.ds(0, 3)], g_s).wait()
+    for g in range(2):
+        sent(u_send.at[g], u_s.at[g])
+        pltpu.make_async_copy(g_send.at[g, pl.ds(0, 3)], g_send.at[g, pl.ds(0, 3)], g_s.at[g]).wait()
 
 
 def local(tokens, w_in, short_taps, skip_bias, filter_spectra, w_out):
     inner_table, first_table, last_table, twist, pick = tables()
     vmem = pl.BlockSpec(memory_space=pltpu.VMEM)
-    smem = pl.BlockSpec(memory_space=pltpu.SMEM)
     hbm = pl.BlockSpec(memory_space=pl.ANY)
     dma = pltpu.SemaphoreType.DMA
     return pl.pallas_call(
         body,
         out_shape=jax.ShapeDtypeStruct((OUT_ROWS, 1024), BF),
-        in_specs=[vmem, hbm, smem, vmem, smem, hbm, hbm, hbm, vmem, vmem, vmem, vmem],
+        in_specs=[hbm] * 11,
         out_specs=vmem,
         scratch_shapes=[
+            pltpu.SMEM((3, 3, CH), F32),
+            pltpu.SMEM((2, CH), F32),
+            pltpu.VMEM((3, 3, CH), F32),
+            pltpu.VMEM((2 * RES, 3 * SEQ), BF),
+            pltpu.VMEM((SEQ, 6 * RES), BF),
+            pltpu.VMEM((2, RES, ROWS), F32),
+            pltpu.VMEM((512, 512), BF),
             pltpu.VMEM((2, 2, 2, ROWS, CH), F32),
             pltpu.VMEM((3, 1024, CH), BF),
             pltpu.VMEM((4, ROWS, ROWS), BF),
             pltpu.VMEM((2, 2 * ROWS, 2 * ROWS), BF),
             pltpu.VMEM((TP, OUT_ROWS, 1024), BF),
-            pltpu.VMEM((TP, CH, 1024), BF),
+            pltpu.VMEM((TP, 2, 128, 1024), BF),
             pltpu.VMEM((4, SEQ, 8, ROWS), BF),
             pltpu.VMEM((4, SEQ, 8, ROWS), BF),
             pltpu.VMEM((SEQ, 8, ROWS), BF),
             pltpu.VMEM((SEQ, 8, ROWS), BF),
-            pltpu.VMEM((SEQ, 4, ROWS), BF),
-            pltpu.VMEM((SEQ, 4, ROWS), BF),
+            pltpu.VMEM((2, SEQ, 2, ROWS), BF),
+            pltpu.VMEM((2, SEQ, 2, ROWS), BF),
             pltpu.VMEM((SEQ, 8, ROWS), F32),
             pltpu.VMEM((ROWS, CH), BF),
             pltpu.VMEM((16, CH), BF),
-            pltpu.VMEM((TP, OUT_ROWS, CH), BF),
-            pltpu.VMEM((TP, OUT_ROWS, CH), BF),
-            dma((4,)),
-            dma((9,)),
+            pltpu.VMEM((ROWS, CH), F32),
+            pltpu.VMEM((2, TP, OUT_ROWS, 128), BF),
+            pltpu.VMEM((2, TP, OUT_ROWS, 128), BF),
+            dma((11,)),
+            dma((12,)),
             dma, dma, dma, dma,
             dma((4,)),
             dma((4,)),
-            dma, dma, dma, dma, dma, dma, dma, dma,
+            dma, dma, dma, dma, dma((2,)), dma((2,)), dma((2,)), dma((2,)),
         ],
         compiler_params=pltpu.CompilerParams(
             collective_id=0, has_side_effects=True, vmem_limit_bytes=60 * 1024 * 1024
         ),
     )(
-        tokens, w_in, short_taps, short_taps, skip_bias, filter_spectra, w_out,
+        tokens, w_in, short_taps, skip_bias, filter_spectra, w_out.reshape(2, 128, 1024),
         jnp.asarray(inner_table), jnp.asarray(first_table), jnp.asarray(last_table),
         jnp.asarray(twist), jnp.asarray(pick),
     )

time: 82.9 us -> 73.7 us (0.89)
  Pallas kernels: 81.1 us -> 72 us
    pallas_call x1, Pallas kernels: 81.1 us -> 72 us  [local(): pl.pallas_call(body, out_shape=jax.ShapeDtypeStruct((OUT_ROWS, 1024), BF)...]
where the time goes in v2:
time: 73.7 us; the launch traced here: 73.6 us
  Pallas kernels  72 us (98%)
  local copies, waits for them, and re-layouts  1.62 us (2%)
    pallas_call x1, Pallas kernels, local(): pl.pallas_call(body, out_shape=jax.ShapeDtypeStruct((OUT_ROWS, 1024), BF)...  72 us
    unnamed x1, local copies, waits for them, and re-layouts  1.62 us

profile of v2, /device:TPU:1, one launch (start us, length us, event | category | flops | bytes accessed | tf_op | source)
XLA Modules:
  0.0 73.6 jit_solution(12021136856907851507)
XLA Ops:
  0.0 72.0 %shard_map.109 = bf16[96,1024]{1,0:T(8,128)(2,1)} custom-call(bf16[96,1024]{1,0:T(8,128)(2,1)} %tok.1, bf16[3,1024,256]{2,1,0:T(8,128)(2,1)} %w_in.1, f32[3,3,256]{2,1,0:T(4,128)} %taps_h.1, f32[2,256]{1,0:T(2,128)} %bias_h.1, f32[2,2,2,384,256]{4,3,2,1,0:T(8,128)} %spec.1, bf16[2,128,1024]{2,1,0:T(8,128)(2,1)} %bitcast.1, ...), custom_call_target="tpu_custom_call" | custom-call | tf_op jit(solution)/shard_map/pallas_call | solution.py:301
  72.0 1.6 %copy.13 = bf16[96,1024]{1,0:T(8,128)(2,1)} copy(bf16[96,1024]{1,0:T(8,128)(2,1)} %shard_map.109) | data formatting | bytes 393216

commit v3 on v2

--- a/solution.py
+++ b/solution.py
@@ -80,19 +80,23 @@
         pl.semaphore_signal(barrier, inc=1, device_id={"seq": peer(i)}, device_id_type=MESH)
         return carry
 
-    lax.fori_loop(1, SEQ, greet, 0)
+    lax.fori_loop(1, SEQ, greet, 0, unroll=7)
     for t in range(1, TP):
         pl.semaphore_signal(barrier, inc=1, device_id={"tp": (mx + t) % TP}, device_id_type=MESH)
 
+    def half(ref, o, g):
+        return ref.at[o, :, :, :, pl.ds(128 * g, 128)]
+
     def loads(k):
         pairs = (
-            (spec.at[0], spec_v.at[0]), (pick_h, pick_c), (w_in, w_in_v), (spec.at[1], spec_v.at[1]),
+            (half(spec, 0, 0), half(spec_v, 0, 0)), (pick_h, pick_c), (half(spec, 0, 1), half(spec_v, 0, 1)),
+            (w_in, w_in_v), (half(spec, 1, 0), half(spec_v, 1, 0)), (half(spec, 1, 1), half(spec_v, 1, 1)),
             (inner_h, inner_v), (first_h, first_c), (twist_h, twist_c), (last_h, last_c),
             (taps_h, taps_v), (taps_h, taps_s), (bias_h, bias_s),
         )
         return pltpu.make_async_copy(pairs[k][0], pairs[k][1], load_sem.at[k])
 
-    for k in range(11):
+    for k in range(13):
         loads(k).start()
 
     def x_copy(src, dst, ssem, rsem, t):
@@ -115,7 +119,7 @@
             ).start()
             return carry
 
-        lax.fori_loop(1, SEQ, one, 0)
+        lax.fori_loop(1, SEQ, one, 0, unroll=7)
         own_copy(send.at[me], recv.at[me], k).start()
 
     def gathered(send, recv, ssem, rsem, k):
@@ -140,19 +144,20 @@
     loads(0).wait()
     loads(1).wait()
     turn_filter(0, 0)
-    turn_filter(0, 1)
     pl.semaphore_wait(barrier, SEQ - 1 + TP - 1)
     for t in range(1, TP):
         x_copy(tok, tg.at[mx], tok_s, tok_r, t).start()
     own_copy(tok, tg.at[mx], 0).start()
     ship_filter(0)
+    loads(2).wait()
+    turn_filter(0, 1)
     ship_filter(1)
 
     for t in range(1, TP):
         x_copy(w_out, wg.at[mx], wo_s, wo_r, t).start()
     own_copy(w_out, wg.at[mx], 1).start()
 
-    loads(2).wait()
+    loads(3).wait()
     own_copy(tok, tg.at[mx], 0).wait()
     pltpu.make_async_copy(tg.at[pl.ds(0, 3)], tg.at[pl.ds(0, 3)], tok_r).wait()
     rows = tg[...].reshape(ROWS, 1024)
@@ -167,12 +172,12 @@
     )
     edge.start()
 
-    loads(3).wait()
-    for g in range(2):
+    for g in range(2):
+        loads(4 + g).wait()
         turn_filter(1, g)
         ship_filter(2 + g)
 
-    for k in range(4, 11):
+    for k in range(6, 13):
         loads(k).wait()
     for part in range(2):
         cos_t = inner_v[2 * part]
@@ -296,7 +301,7 @@
 def local(tokens, w_in, short_taps, skip_bias, filter_spectra, w_out):
     inner_table, first_table, last_table, twist, pick = tables()
     vmem = pl.BlockSpec(memory_space=pltpu.VMEM)
-    hbm = pl.BlockSpec(memory_space=pl.ANY)
+    hbm = pl.BlockSpec(memory_space=pltpu.HBM)
     dma = pltpu.SemaphoreType.DMA
     return pl.pallas_call(
         body,
@@ -329,7 +334,7 @@
             pltpu.VMEM((ROWS, CH), F32),
             pltpu.VMEM((2, TP, OUT_ROWS, 128), BF),
             pltpu.VMEM((2, TP, OUT_ROWS, 128), BF),
-            dma((11,)),
+            dma((13,)),
             dma((12,)),
             dma, dma, dma, dma,
             dma((4,)),
@@ -337,12 +342,14 @@
             dma, dma, dma, dma, dma((2,)), dma((2,)), dma((2,)), dma((2,)),
         ],
         compiler_params=pltpu.CompilerParams(
-            collective_id=0, has_side_effects=True, vmem_limit_bytes=60 * 1024 * 1024
+            collective_id=0, has_side_effects=True, vmem_limit_bytes=40 * 1024 * 1024
         ),
     )(
+        *[pltpu.with_memory_space_constraint(item, pltpu.HBM) for item in (
         tokens, w_in, short_taps, skip_bias, filter_spectra, w_out.reshape(2, 128, 1024),
         jnp.asarray(inner_table), jnp.asarray(first_table), jnp.asarray(last_table),
         jnp.asarray(twist), jnp.asarray(pick),
+            )]
     )
 
 

time: 73.7 us -> 72 us (0.977)
  local copies, waits for them, and re-layouts: 1.62 us -> 0.68 us
  Pallas kernels: 72 us -> 71.2 us
    unnamed x1, local copies, waits for them, and re-layouts: 1.62 us -> 0.68 us
    pallas_call x1, Pallas kernels: 72 us -> 71.2 us  [local(): pl.pallas_call(body, out_shape=jax.ShapeDtypeStruct((OUT_ROWS, 1024), BF)...]
where the time goes in v3:
time: 72 us; the launch traced here: 71.9 us
  Pallas kernels  71.2 us (99%)
    pallas_call x1, Pallas kernels, local(): pl.pallas_call(body, out_shape=jax.ShapeDtypeStruct((OUT_ROWS, 1024), BF)...  71.2 us

profile of v3, /device:TPU:1, one launch (start us, length us, event | category | flops | bytes accessed | tf_op | source)
XLA Modules:
  0.0 71.9 jit_solution(3785544091158701018)
XLA Ops:
  0.0 71.2 %shard_map.109 = bf16[96,1024]{1,0:T(8,128)(2,1)S(1)} custom-call(bf16[96,1024]{1,0:T(8,128)(2,1)} %tok.1, bf16[3,1024,256]{2,1,0:T(8,128)(2,1)} %w_in.1, f32[3,3,256]{2,1,0:T(4,128)} %taps_h.1, f32[2,256]{1,0:T(2,128)} %bias_h.1, f32[2,2,2,384,256]{4,3,2,1,0:T(8,128)} %spec.1, bf16[2,128,1024]{2,1,0:T(8,128)(2,1)} %bitcast.1, ...), custom_call_target="tpu_custom_call" | custom-call | tf_op jit(solution)/shard_map/pallas_call | solution.py:306
  71.2 0.7 copy.13

commit v4 on v3

--- a/solution.py
+++ b/solution.py
@@ -217,14 +217,15 @@
                 hr = wide[:, j * 2 + low, :]
                 hi = wide[:, (2 + j) * 2 + low, :]
                 blocks.append(jnp.concatenate([xr * hr - xi * hi, xr * hi + xi * hr], axis=1))
-        v = thrice(jnp.concatenate(blocks, axis=0), NT)
+        lines_in = jnp.concatenate(blocks, axis=0)
+        v = thrice(lines_in, NT) if k < 2 else dot(lines_in.astype(BF), wmat[0], NT)
         real, imag = [], []
         for low in range(2):
             vr, vi = v[RES * low : RES * low + RES, :ROWS], v[RES * low : RES * low + RES, ROWS:]
             real.append(vr * tr + vi * ti)
             imag.append(vi * tr - vr * ti)
         rhs = jnp.concatenate([jnp.concatenate(real, axis=1), jnp.concatenate(imag, axis=1)], axis=0)
-        y = dot(last_c[...], stacked(rhs))
+        y = dot(last_c[...], stacked(rhs)) if k < 2 else dot(last_c[:, : 2 * RES], rhs.astype(BF))
         return [y[:, :ROWS], y[:, ROWS:]]
 
     at_row = lax.broadcasted_iota(jnp.int32, (SEQ, ROWS), 0)
@@ -275,7 +276,7 @@
         turned = jnp.concatenate([wide[:, low, :] for low in range(2)], axis=0).T
         lanes = slice(128 * g, 128 * g + 128)
         g_send[g] = (gate_v[:, lanes] * turned).astype(BF).reshape(TP, OUT_ROWS, 128)
-        for t in range(1, TP):
+        for t in (2, 1, 3):
             x_copy(g_send.at[g, (mx + t) % TP], g_recv.at[g, mx], g_s.at[g], g_r.at[g], t).start()
         own_copy(g_send.at[g, mx], g_recv.at[g, mx], 10 + g).start()
     own_copy(w_out, wg.at[mx], 1).wait()

time: 72 us -> 71.1 us (0.987)
  Pallas kernels: 71.2 us -> 70.3 us
    pallas_call x1, Pallas kernels: 71.2 us -> 70.3 us  [local(): pl.pallas_call(body, out_shape=jax.ShapeDtypeStruct((OUT_ROWS, 1024), BF)...]
where the time goes in v4:
time: 71.1 us; the launch traced here: 71 us
  Pallas kernels  70.3 us (99%)
    pallas_call x1, Pallas kernels, local(): pl.pallas_call(body, out_shape=jax.ShapeDtypeStruct((OUT_ROWS, 1024), BF)...  70.3 us

profile of v4, /device:TPU:1, one launch (start us, length us, event | category | flops | bytes accessed | tf_op | source)
XLA Modules:
  0.0 71.0 jit_solution(2477271114065639326)
XLA Ops:
  0.0 70.3 %shard_map.109 = bf16[96,1024]{1,0:T(8,128)(2,1)S(1)} custom-call(bf16[96,1024]{1,0:T(8,128)(2,1)} %tok.1, bf16[3,1024,256]{2,1,0:T(8,128)(2,1)} %w_in.1, f32[3,3,256]{2,1,0:T(4,128)} %taps_h.1, f32[2,256]{1,0:T(2,128)} %bias_h.1, f32[2,2,2,384,256]{4,3,2,1,0:T(8,128)} %spec.1, bf16[2,128,1024]{2,1,0:T(8,128)(2,1)} %bitcast.1, ...), custom_call_target="tpu_custom_call" | custom-call | tf_op jit(solution)/shard_map/pallas_call | solution.py:307
  70.3 0.7 copy.13

commit v5 on v4

--- a/solution.py
+++ b/solution.py
@@ -119,7 +119,7 @@
             ).start()
             return carry
 
-        lax.fori_loop(1, SEQ, one, 0, unroll=7)
+        lax.fori_loop(1, SEQ, one, 0, unroll=63 if k >= 8 else 7)
         own_copy(send.at[me], recv.at[me], k).start()
 
     def gathered(send, recv, ssem, rsem, k):

time: 71.1 us -> 71 us (level)
  no operation moved by 1% of the time
where the time goes in v5:
time: 71 us
  Pallas kernels  70.3 us (99%)
    pallas_call x1, Pallas kernels, local(): pl.pallas_call(body, out_shape=jax.ShapeDtypeStruct((OUT_ROWS, 1024), BF)...  70.3 us

profile of v5, /device:TPU:1, one launch (start us, length us, event | category | flops | bytes accessed | tf_op | source)
XLA Modules:
  0.0 71.0 jit_solution(9969991968569293380)
XLA Ops:
  0.0 70.3 %shard_map.109 = bf16[96,1024]{1,0:T(8,128)(2,1)S(1)} custom-call(bf16[96,1024]{1,0:T(8,128)(2,1)} %tok.1, bf16[3,1024,256]{2,1,0:T(8,128)(2,1)} %w_in.1, f32[3,3,256]{2,1,0:T(4,128)} %taps_h.1, f32[2,256]{1,0:T(2,128)} %bias_h.1, f32[2,2,2,384,256]{4,3,2,1,0:T(8,128)} %spec.1, bf16[2,128,1024]{2,1,0:T(8,128)(2,1)} %bitcast.1, ...), custom_call_target="tpu_custom_call" | custom-call | tf_op jit(solution)/shard_map/pallas_call | solution.py:307
  70.3 0.7 copy.13

commit v6 on v5

--- a/solution.py
+++ b/solution.py
@@ -80,7 +80,7 @@
         pl.semaphore_signal(barrier, inc=1, device_id={"seq": peer(i)}, device_id_type=MESH)
         return carry
 
-    lax.fori_loop(1, SEQ, greet, 0, unroll=7)
+    lax.fori_loop(1, SEQ, greet, 0, unroll=63)
     for t in range(1, TP):
         pl.semaphore_signal(barrier, inc=1, device_id={"tp": (mx + t) % TP}, device_id_type=MESH)
 

time: 71 us -> 71 us (level)
  no operation moved by 1% of the time
where the time goes in v6:
time: 71 us
  Pallas kernels  70.3 us (99%)
    pallas_call x1, Pallas kernels, local(): pl.pallas_call(body, out_shape=jax.ShapeDtypeStruct((OUT_ROWS, 1024), BF)...  70.3 us

profile of v6, /device:TPU:1, one launch (start us, length us, event | category | flops | bytes accessed | tf_op | source)
XLA Modules:
  0.0 71.0 jit_solution(16350397342463466169)
XLA Ops:
  0.0 70.3 %shard_map.109 = bf16[96,1024]{1,0:T(8,128)(2,1)S(1)} custom-call(bf16[96,1024]{1,0:T(8,128)(2,1)} %tok.1, bf16[3,1024,256]{2,1,0:T(8,128)(2,1)} %w_in.1, f32[3,3,256]{2,1,0:T(4,128)} %taps_h.1, f32[2,256]{1,0:T(2,128)} %bias_h.1, f32[2,2,2,384,256]{4,3,2,1,0:T(8,128)} %spec.1, bf16[2,128,1024]{2,1,0:T(8,128)(2,1)} %bitcast.1, ...), custom_call_target="tpu_custom_call" | custom-call | tf_op jit(solution)/shard_map/pallas_call | solution.py:307
  70.3 0.7 copy.13
